TPU v7x, 32 devices: a whole 2x2x4 slice. The times are simulated.
32 devices in a mesh: groups: 2 (over y), dp: 4 (over z), feat: 2 (over core), ens: 2 (over x).
Axes of the slice: x: 2, y: 2, z: 4, core: 2. Of those that a mesh axis runs over, the one named last changes fastest.
Arguments:
- test_feat: bfloat16 [2, 64, 8192], P('ens', 'groups', 'dp'), parts along dimension 1, may hold values from -6 to 6
- kernel_inverse: bfloat16 [2, 8192, 8192], P('ens', 'dp', 'feat'), may hold values from -0.0625 to 0.0625
- train_feat: bfloat16 [2, 1024, 8192], P('ens', 'dp', 'feat'), may hold values from -0.0625 to 0.0625
- residual_weight: float32 [2, 1024], P('ens', 'dp'), may hold values from 0.05 to 1
Outputs:
- scores: float32 [64, 1024], P(('groups', 'feat', 'ens'), 'dp'), parts along dimension 0
There are 2 independent parts, one for each index of `groups`. A program takes and returns all parts, laid end to end along the dimension named above; an argument that names none is the same for every part. Nothing has to cross between parts.
All inputs are finite; a program needn't handle non-finite values.
Results may differ from a plain program's by a relative error of at most 0.0029.
Values may be sent and summed in bfloat16 or wider, within the bound.
A program may use at most 64 MiB of HBM per device.

v0:
```python
import jax
import jax.numpy as jnp
from jax import lax
from jax.sharding import PartitionSpec as P


def shards(test_feat, kernel_inverse, train_feat, residual_weight):
    test_local = test_feat[0]
    inverse_local = kernel_inverse[0]
    train_local = train_feat[0]
    weight_row = residual_weight[0][None, :]
    partial_sum = jnp.dot(test_local, inverse_local, preferred_element_type=jnp.float32)
    projected = lax.psum(partial_sum, "dp").astype(jnp.bfloat16)
    raw = jnp.einsum("tf,nf->tn", projected, train_local, preferred_element_type=jnp.float32)
    totals = raw * weight_row
    return lax.psum_scatter(totals, ("feat", "ens"), scatter_dimension=0, tiled=True)


def solution(mesh):
    in_specs = (
        P("ens", "groups", "dp"),
        P("ens", "dp", "feat"),
        P("ens", "dp", "feat"),
        P("ens", "dp"),
    )
    out_specs = P(("groups", "feat", "ens"), "dp")
    return jax.shard_map(shards, mesh=mesh, in_specs=in_specs, out_specs=out_specs, check_vma=False)
```

profile of v0, /device:TPU:0, one launch (start us, length us, event | category | flops | bytes accessed | tf_op | source)
XLA Modules:
  0.0 74.1 jit_solution(5447746823196072305)
XLA Ops:
  6.5 0.0 copy-start
  6.5 0.0 copy-start.1
  6.5 0.0 reduce-scatter.2.cloned.1.call-start
  6.5 9.0 %fusion = f32[32,4096]{1,0:T(8,128)S(1)} fusion(bf16[1,2048,4096]{2,1,0:T(8,128)(2,1)} %param.5, bf16[1,32,2048]{2,1,0:T(8,128)(2,1)} %param.4), kind=kOutput, calls=%fused_computation | convolution fusion | flops 536870912 | bytes 17432576 | tf_op jit(solution)/shard_map/dot_general | solution.py:12
  15.5 32.1 %all-reduce.1 = bf16[32,4096]{1,0:T(8,128)(2,1)S(1)} all-reduce(f32[32,4096]{1,0:T(8,128)S(1)} %fusion), channel_id=1, replica_groups=mesh['groups'=2,'dp'=4,'feat'=2,'ens'=2] {'dp'}, use_global_device_ids=true, to_apply=%region_0.0 | all-reduce | flops 131072 | bytes 786432 | tf_op jit(solution)/shard_map/psum | solution.py:13
  47.6 0.0 copy-done
  47.6 0.0 copy-done.1
  47.6 1.3 %fusion.4 = f32[32,256]{1,0:T(8,128)} fusion(bf16[1,256,4096]{2,1,0:T(8,128)(2,1)S(1)} %copy-done, bf16[32,4096]{1,0:T(8,128)(2,1)S(1)} %all-reduce.1, f32[256]{0:T(256)S(1)} %bitcast.13), kind=kOutput, calls=%fused_computation.4 | convolution fusion | flops 67117056 | bytes 2393088 | tf_op jit(solution)/shard_map/tf,nf->tn/dot_general | solution.py:14
  49.0 0.0 reduce-scatter.2.cloned.1.call-update
  49.0 18.2 %reduce-scatter.2.cloned.1.call-done = f32[8,256]{1,0:T(8,128)} async-done(((f32[32,256]{1,0:T(8,128)}), f32[8,256]{1,0:T(8,128)}) %reduce-scatter.2.cloned.1.call-update) | async-done | bytes 8208 | tf_op jit(solution)/shard_map/reduce_scatter | solution.py:16
Async XLA Ops:
  6.5 41.1 %copy-start = (bf16[1,256,4096]{2,1,0:T(8,128)(2,1)S(1)}, bf16[1,256,4096]{2,1,0:T(8,128)(2,1)}, u32[]{:S(2)}) copy-start(bf16[1,256,4096]{2,1,0:T(8,128)(2,1)} %param.6) | copy-start | bytes 6291460
  6.5 41.1 %copy-start.1 = (f32[1,256]{1,0:T(1,128)S(1)}, f32[1,256]{1,0:T(1,128)}, u32[]{:S(2)}) copy-start(f32[1,256]{1,0:T(1,128)} %param.7) | copy-start | bytes 3076
  6.5 60.7 %reduce-scatter.2.cloned.1.call-start = ((), (), s32[]{:S(2)}) async-start(), calls=%async_computation.1 | async-start | bytes 40960 | tf_op jit(solution)/shard_map/reduce_scatter | solution.py:16
Sparse Core Ops, SparseCore 0:
  49.1 18.0 reduce-scatter.1
where the time goes:
time: 74.3 us; the launch traced here: 74.1 us
  blocking collectives  32.1 us (43%)
  waiting for transfers between devices  18.3 us (25%)
  between operations  13.4 us (18%)
  matrix products  10.3 us (14%)
    psum x1, blocking collectives, shards(): projected = lax.psum(partial_sum, 'dp').astype(jnp.bfloat16)  32.1 us
    reduce_scatter x1, waiting for transfers between devices, shards(): lax.psum_scatter(totals, ('feat', 'ens'), scatter_dimension=0, tiled=True)  18.2 us
    dot_general x1, matrix products, shards(): jnp.dot(test_local, inverse_local, preferred_element_type=jnp.float32)  8.96 us
  transfers between devices with their start and end apart: 1, of which 1 were waited for; matrix products, arithmetic and copies ran while one was open for 0% of the time, Pallas kernels for 0%

commit v1 on v0

--- a/solution.py
+++ b/solution.py
@@ -10,7 +10,7 @@
     train_local = train_feat[0]
     weight_row = residual_weight[0][None, :]
     partial_sum = jnp.dot(test_local, inverse_local, preferred_element_type=jnp.float32)
-    projected = lax.psum(partial_sum, "dp").astype(jnp.bfloat16)
+    projected = jnp.sum(lax.all_gather(partial_sum, "dp"), axis=0).astype(jnp.bfloat16)
     raw = jnp.einsum("tf,nf->tn", projected, train_local, preferred_element_type=jnp.float32)
     totals = raw * weight_row
     return lax.psum_scatter(totals, ("feat", "ens"), scatter_dimension=0, tiled=True)

time: 74.3 us -> 93.5 us (1.26)
  waiting for transfers between devices: 18.3 us -> 67 us
  blocking collectives: 32.1 us -> 0 us
  other arithmetic: 0 us -> 1.75 us
    all_gather x0 -> x1, waiting for transfers between devices: none -> 48.5 us  [shards(): lax.all_gather(partial_sum, 'dp')]
    psum x1 -> x0, blocking collectives: 32.1 us -> none  [shards(): projected = lax.psum(partial_sum, 'dp').astype(jnp.bfloat16)]
    reduce_sum x0 -> x1, other arithmetic: none -> 1.75 us  [shards(): jnp.sum(lax.all_gather(partial_sum, 'dp'), axis=0).astype(jnp.bfloat16)]
  transfers between devices with their start and end apart: 1 -> 2, of which waited for: 1 -> 2; matrix products, arithmetic and copies ran while one was open for 0% -> 0% of each run, Pallas kernels for 0% -> 0%
where the time goes in v1:
time: 93.5 us; the launch traced here: 93.3 us
  waiting for transfers between devices  67 us (72%)
  between operations  13.4 us (14%)
  matrix products  11.1 us (12%)
  other arithmetic  1.75 us (2%)
    all_gather x1, waiting for transfers between devices, shards(): lax.all_gather(partial_sum, 'dp')  48.5 us
    reduce_scatter x1, waiting for transfers between devices, shards(): lax.psum_scatter(totals, ('feat', 'ens'), scatter_dimension=0, tiled=True)  18.5 us
    dot_general x1, matrix products, shards(): jnp.dot(test_local, inverse_local, preferred_element_type=jnp.float32)  9.76 us
  transfers between devices with their start and end apart: 2, of which 2 were waited for; matrix products, arithmetic and copies ran while one was open for 0% of the time, Pallas kernels for 0%

profile of v1, /device:TPU:0, one launch (start us, length us, event | category | flops | bytes accessed | tf_op | source)
XLA Modules:
  0.0 93.3 jit_solution(13089435950425511893)
XLA Ops:
  6.5 0.0 copy-start
  6.5 0.0 all-gather.3.cloned.1.call-start
  6.5 9.8 %fusion = f32[32,4096]{1,0:T(8,128)} fusion(bf16[1,2048,4096]{2,1,0:T(8,128)(2,1)} %param.5, bf16[1,32,2048]{2,1,0:T(8,128)(2,1)} %param.4), kind=kOutput, calls=%fused_computation | convolution fusion | flops 536870912 | bytes 17432576 | tf_op jit(solution)/shard_map/dot_general | solution.py:12
  16.3 0.0 copy-start.1
  16.3 0.0 all-gather.3.cloned.1.call-update
  16.3 0.0 reduce-scatter.2.cloned.1.call-start
  16.4 48.5 %all-gather.3.cloned.1.call-done = f32[128,4096]{1,0:T(8,128)} async-done(((f32[32,4096]{1,0:T(8,128)}), f32[128,4096]{1,0:T(8,128)}) %all-gather.3.cloned.1.call-update) | async-done | bytes 2097168 | tf_op jit(solution)/shard_map/all_gather | solution.py:13
  64.9 1.7 %reduce_sum.9 = bf16[32,4096]{1,0:T(8,128)(2,1)S(1)} reduce(f32[4,32,4096]{2,1,0:T(8,128)} %bitcast.14, f32[]{:T(128)} %constant.0.clone.1), dimensions={0}, to_apply=%region_0.0 | reduce | flops 393216 | bytes 2359300 | tf_op jit(solution)/shard_map/reduce_sum | solution.py:13
  66.6 0.0 copy-done
  66.6 0.0 copy-done.1
  66.6 1.4 %fusion.4 = f32[32,256]{1,0:T(8,128)} fusion(bf16[1,256,4096]{2,1,0:T(8,128)(2,1)S(1)} %copy-done, bf16[32,4096]{1,0:T(8,128)(2,1)S(1)} %reduce_sum.9, f32[256]{0:T(256)S(1)} %bitcast.15), kind=kOutput, calls=%fused_computation.4 | convolution fusion | flops 67117056 | bytes 2393088 | tf_op jit(solution)/shard_map/tf,nf->tn/dot_general | solution.py:14
  68.0 0.0 reduce-scatter.2.cloned.1.call-update
  68.0 18.5 %reduce-scatter.2.cloned.1.call-done = f32[8,256]{1,0:T(8,128)} async-done(((f32[32,256]{1,0:T(8,128)}), f32[8,256]{1,0:T(8,128)}) %reduce-scatter.2.cloned.1.call-update) | async-done | bytes 8208 | tf_op jit(solution)/shard_map/reduce_scatter | solution.py:16
Async XLA Ops:
  6.5 60.1 %copy-start = (bf16[1,256,4096]{2,1,0:T(8,128)(2,1)S(1)}, bf16[1,256,4096]{2,1,0:T(8,128)(2,1)}, u32[]{:S(2)}) copy-start(bf16[1,256,4096]{2,1,0:T(8,128)(2,1)} %param.6) | copy-start | bytes 6291460
  6.5 58.3 %all-gather.3.cloned.1.call-start = ((), (), s32[]{:S(2)}) async-start(), calls=%async_computation.2 | async-start | bytes 2621440 | tf_op jit(solution)/shard_map/all_gather | solution.py:13
  16.3 50.3 %copy-start.1 = (f32[1,256]{1,0:T(1,128)S(1)}, f32[1,256]{1,0:T(1,128)}, u32[]{:S(2)}) copy-start(f32[1,256]{1,0:T(1,128)} %param.7) | copy-start | bytes 3076
  16.3 70.2 %reduce-scatter.2.cloned.1.call-start = ((), (), s32[]{:S(2)}) async-start(), calls=%async_computation.1 | async-start | bytes 40960 | tf_op jit(solution)/shard_map/reduce_scatter | solution.py:16
Sparse Core Ops, SparseCore 0:
  16.4 48.3 all-gather.2
  68.1 18.3 reduce-scatter.1
